TPU v7x, 512 devices: a whole 4x8x8 slice. The times are simulated.
512 devices in a mesh: lev: 8 (over z_lo, core), tile: 64 (over z_hi, y, x).
Axes of the slice: x: 4, y: 8, z: 8 (z_hi: 2, z_lo: 4; z = z_hi * 4 + z_lo), core: 2. Of those that a mesh axis runs over, the one named last changes fastest.
Arguments:
- adjoint: float32 [5, 64, 1024, 256], P(None, 'lev', 'tile'), may hold values from -6 to 6
- courant: float32 [2, 64, 1024, 256], P(None, 'lev', 'tile'), may hold values from -0.6 to 0.6
- metric: float32 [2, 64, 1024, 256], P(None, 'lev', 'tile'), may hold values from 0.5 to 2
- pivot_inverse: float32 [4, 64, 1024, 256], P(None, 'lev', 'tile'), may hold values from -0.06 to 0.2
- lower_gain: float32 [4, 64, 1024, 256], P(None, 'lev', 'tile'), may hold values from -0.5 to 1
- upper_gain: float32 [4, 64, 1024, 256], P(None, 'lev', 'tile'), may hold values from -0.5 to 1
Outputs:
- stepped: float32 [5, 64, 1024, 256], P(None, 'lev', 'tile')
All inputs are finite; a program needn't handle non-finite values.
Results may differ from a plain program's by a relative error of at most 0.00002.
Values sent between devices are 32-bit elements; how exact they have to be, the bound alone decides.
A program may use at most 64 MiB of HBM per device.

v0:
```python
import jax
import jax.numpy as jnp
from jax import lax
from jax.sharding import PartitionSpec as P

LEVEL_UNROLL = 16


def with_halo(block, sides, width):
    for axis, dim in sides:
        count = lax.axis_size(axis)
        forward = [(i, i + 1) for i in range(count - 1)]
        forward.append((count - 1, 0))
        backward = [(target, source) for source, target in forward]
        low = lax.ppermute(
            lax.slice_in_dim(block, block.shape[dim] - width, None, axis=dim), axis, forward
        )
        high = lax.ppermute(lax.slice_in_dim(block, 0, width, axis=dim), axis, backward)
        block = jnp.concatenate([low, block, high], axis=dim)
    return block


def centered_roll(values, axis_id):
    ahead_one = jnp.roll(values, -1, axis_id)
    behind_one = jnp.roll(values, 1, axis_id)
    ahead_two = jnp.roll(values, -2, axis_id)
    behind_two = jnp.roll(values, 2, axis_id)
    return (8.0 * (ahead_one - behind_one) - (ahead_two - behind_two)) / 12.0


def centered_padded(padded):
    ahead_one = padded[:, :, 3:-1, :]
    behind_one = padded[:, :, 1:-3, :]
    ahead_two = padded[:, :, 4:, :]
    behind_two = padded[:, :, :-4, :]
    return (8.0 * (ahead_one - behind_one) - (ahead_two - behind_two)) / 12.0


def mat_vec(system_matrix, vector):
    return jnp.stack(
        [
            system_matrix[0] * vector[0] + system_matrix[1] * vector[1],
            system_matrix[2] * vector[0] + system_matrix[3] * vector[1],
        ]
    )


def chain_run(coupling, forcing, initial, backward):

    def advance(state, inputs):
        fresh = mat_vec(inputs[0], state) + inputs[1]
        return (fresh, fresh)

    final_state, states = lax.scan(
        advance,
        initial,
        (jnp.moveaxis(coupling, 1, 0), jnp.moveaxis(forcing, 1, 0)),
        reverse=backward,
        unroll=min(LEVEL_UNROLL, coupling.shape[1]),
    )
    return jnp.moveaxis(states, 0, 1)


def column_solve(pieces):
    forcing, lower_part, upper_part = pieces
    initial = jnp.zeros((2,) + forcing.shape[2:], jnp.float32)
    lowered = chain_run(lower_part, forcing, initial, False)
    solved = chain_run(upper_part, lowered, initial, True)
    return lax.all_to_all(solved, "lev", split_axis=1, concat_axis=2, tiled=True)


def local(adjoint, courant, metric, pivot_inverse, lower_gain, upper_gain):
    weighted = jnp.concatenate([courant[0] * adjoint, (metric[0] * adjoint[0])[None]], 0)
    padded = with_halo(weighted, (("tile", 2),), 2)
    across = centered_padded(padded)
    advected = adjoint + across[:5] + centered_roll(courant[1] * adjoint, 3)
    pressure_field = advected[4] + across[5] + centered_roll(metric[1] * adjoint[1], 2)
    forcing = mat_vec(pivot_inverse, jnp.stack([advected[2], pressure_field]))
    solved = column_solve(
        (
            lax.all_to_all(forcing, "lev", split_axis=2, concat_axis=1, tiled=True),
            lax.all_to_all(lower_gain, "lev", split_axis=2, concat_axis=1, tiled=True),
            lax.all_to_all(upper_gain, "lev", split_axis=2, concat_axis=1, tiled=True),
        )
    )
    return jnp.stack([advected[0], advected[1], solved[0], advected[3], solved[1]])


def solution(mesh):
    placed = (
        P(None, "lev", "tile", None),
        P(None, "lev", "tile", None),
        P(None, "lev", "tile", None),
        P(None, "lev", "tile", None),
        P(None, "lev", "tile", None),
        P(None, "lev", "tile", None),
    )
    return jax.shard_map(
        local, mesh=mesh, in_specs=placed, out_specs=P(None, "lev", "tile", None), check_vma=False
    )
```

profile of v0, /device:TPU:1, one launch (start us, length us, event | category | flops | bytes accessed | tf_op | source)
XLA Modules:
  0.0 111.3 jit_solution(6777337082465802634)
XLA Ops:
  0.0 1.1 slice_bitcast_fusion.4
  1.1 1.1 %multiply_bitcast_fusion = (f32[8,16,256]{2,1,0:T(8,128)S(1)}, f32[1,8,16,256]{3,2,1,0:T(8,128)S(1)}) fusion(f32[5,8,16,256]{3,2,1,0:T(8,128)} %param.10, f32[2,8,16,256]{3,2,1,0:T(8,128)} %param.12), kind=kLoop, calls=%fused_computation.612 | loop fusion | flops 65536 | bytes 786432 | tf_op jit(solution)/shard_map/mul | solution.py:77
  2.2 0.1 broadcast_multiply_fusion
  2.4 16.6 %collective-permute-start = (f32[6,8,2,256]{3,1,2,0:T(8,128)S(1)}, f32[6,8,2,256]{3,1,2,0:T(8,128)S(1)}, u32[]{:S(2)}, u32[]{:S(2)}) collective-permute-start(f32[6,8,2,256]{3,1,2,0:T(8,128)S(1)} %copy.304), channel_id=1, source_target_pairs={{1,0},{2,1},{3,2},{4,3},{5,4},{6,5},{7,6},{8,7},{9,8},{10,9},{11,1... | collective-permute-start | bytes 294920 | tf_op jit(solution)/shard_map/ppermute | solution.py:18
  19.0 1.9 %collective-permute-start.1 = (f32[6,8,2,256]{3,1,2,0:T(8,128)S(1)}, f32[6,8,2,256]{3,1,2,0:T(8,128)S(1)}, u32[]{:S(2)}, u32[]{:S(2)}) collective-permute-start(f32[6,8,2,256]{3,1,2,0:T(8,128)S(1)} %copy.305), channel_id=1, source_target_pairs={{0,1},{1,2},{2,3},{3,4},{4,5},{5,6},{6,7},{7,8},{8,9},{9,10},{10,1... | collective-permute-start | bytes 294920 | tf_op jit(solution)/shard_map/ppermute | solution.py:15
  20.9 0.2 fusion.206
  21.2 0.2 fusion.208
  21.4 0.2 fusion.205
  21.6 0.2 fusion.207
  21.7 0.1 slice_bitcast_fusion.3
  21.8 0.1 slice_bitcast_fusion.1
  22.2 11.5 %collective-permute-done.1 = f32[6,8,2,256]{3,1,2,0:T(8,128)S(1)} collective-permute-done((f32[6,8,2,256]{3,1,2,0:T(8,128)S(1)}, f32[6,8,2,256]{3,1,2,0:T(8,128)S(1)}, u32[]{:S(2)}, u32[]{:S(2)}) %collective-permute-start.1) | collective-permute-done | bytes 98336 | tf_op jit(solution)/shard_map/ppermute | solution.py:15
  33.7 0.2 pad_maximum_fusion
  33.9 0.3 fusion.193
  34.2 0.6 fusion.195
  34.9 0.4 copy-done.2
  35.3 0.2 multiply_add_fusion.1
  35.5 0.8 copy.287
  36.4 6.2 %all-to-all-start.2 = ((f32[2,8,16,256]{3,1,0,2:T(8,128)}), f32[2,8,16,256]{3,1,0,2:T(8,128)S(1)}, u32[]{:S(2)}, u32[]{:S(2)}) async-start(f32[2,8,16,256]{3,1,0,2:T(8,128)} %copy.287), calls=%async_computation.2 | async-start | bytes 524288 | tf_op jit(solution)/shard_map/all_to_all | solution.py:81
  42.6 1.1 copy.282
  43.7 7.6 %all-to-all-done.2 = f32[2,8,16,256]{3,1,0,2:T(8,128)S(1)} async-done(((f32[2,8,16,256]{3,1,0,2:T(8,128)}), f32[2,8,16,256]{3,1,0,2:T(8,128)S(1)}, u32[]{:S(2)}, u32[]{:S(2)}) %all-to-all-start.2) | async-done | bytes 262176 | tf_op jit(solution)/shard_map/all_to_all | solution.py:81
  51.3 4.4 %all-to-all-start.1 = ((f32[4,8,16,256]{3,1,0,2:T(8,128)}), f32[4,8,16,256]{3,1,0,2:T(8,128)S(1)}, u32[]{:S(2)}, u32[]{:S(2)}) async-start(f32[4,8,16,256]{3,1,0,2:T(8,128)} %copy.282), calls=%async_computation.1 | async-start | bytes 1048576 | tf_op jit(solution)/shard_map/all_to_all | solution.py:82
  55.8 1.1 copy.279
  56.9 13.3 %all-to-all-done.1 = f32[4,8,16,256]{3,1,0,2:T(8,128)S(1)} async-done(((f32[4,8,16,256]{3,1,0,2:T(8,128)}), f32[4,8,16,256]{3,1,0,2:T(8,128)S(1)}, u32[]{:S(2)}, u32[]{:S(2)}) %all-to-all-start.1) | async-done | bytes 524320 | tf_op jit(solution)/shard_map/all_to_all | solution.py:82
  70.2 4.4 %all-to-all-start = ((f32[4,8,16,256]{3,1,0,2:T(8,128)}), f32[4,8,16,256]{3,1,0,2:T(8,128)S(1)}, u32[]{:S(2)}, u32[]{:S(2)}) async-start(f32[4,8,16,256]{3,1,0,2:T(8,128)} %copy.279), calls=%async_computation | async-start | bytes 1048576 | tf_op jit(solution)/shard_map/all_to_all | solution.py:83
  74.6 5.3 %while.30 = (s32[]{:T(128)}, f32[2,2,256]{2,1,0:T(2,128)S(1)}, f32[4,16,2,2,256]{4,3,2,1,0:T(2,128)S(1)}, f32[4,16,4,2,256]{4,1,0,3,2:T(8,128)S(1)}, f32[4,16,2,...) while((s32[]{:T(128)}, f32[2,2,256]{2,1,0:T(2,128)S(1)}, ...), condition=%wide.region_1.2_spmd.clone, body=%wide.region_0.1_spmd.clone.sunk | while | flops 115729 | bytes 1188359 | solution.py:54
  74.7 0.4 constant_dynamic-slice_fusion.163
  75.1 0.1 constant_dynamic-slice_fusion.164
  76.0 0.4 constant_dynamic-slice_fusion.163
  76.4 0.1 constant_dynamic-slice_fusion.164
  77.3 0.4 constant_dynamic-slice_fusion.163
  77.7 0.1 constant_dynamic-slice_fusion.164
  78.6 0.4 constant_dynamic-slice_fusion.163
  79.1 0.1 constant_dynamic-slice_fusion.164
  79.9 9.0 %all-to-all-done = f32[4,8,16,256]{3,1,0,2:T(8,128)S(1)} async-done(((f32[4,8,16,256]{3,1,0,2:T(8,128)}), f32[4,8,16,256]{3,1,0,2:T(8,128)S(1)}, u32[]{:S(2)}, u32[]{:S(2)}) %all-to-all-start) | async-done | bytes 524320 | tf_op jit(solution)/shard_map/all_to_all | solution.py:83
  89.0 0.8 broadcast.22
  89.7 7.5 %while.31 = (s32[]{:T(128)}, f32[2,2,256]{2,1,0:T(2,128)S(1)}, f32[4,16,2,2,256]{4,3,2,1,0:T(2,128)}, f32[4,16,4,2,256]{4,1,0,3,2:T(8,128)S(1)}, f32[4,16,2,2,25...) while((s32[]{:T(128)}, f32[2,2,256]{2,1,0:T(2,128)S(1)}, ...), condition=%wide.region_3.4_spmd.clone, body=%wide.region_2.3_spmd.clone.sunk | while | flops 115730 | bytes 1057491 | solution.py:54
  89.7 0.1 constant_dynamic-slice_fusion.165
  90.8 0.6 bitcast_dynamic-update-slice_fusion.5
  91.4 0.3 constant_dynamic-slice_fusion.165
  92.7 0.6 bitcast_dynamic-update-slice_fusion.5
  93.4 0.3 constant_dynamic-slice_fusion.165
  94.7 0.6 bitcast_dynamic-update-slice_fusion.5
  95.3 0.3 constant_dynamic-slice_fusion.165
  96.6 0.6 bitcast_dynamic-update-slice_fusion.5
  97.2 4.3 %all-to-all-start.3 = ((f32[2,64,2,256]{3,2,0,1:T(2,128)}), f32[2,64,2,256]{3,2,0,1:T(2,128)S(1)}, u32[]{:S(2)}, u32[]{:S(2)}) async-start(f32[2,64,2,256]{3,2,0,1:T(2,128)} %bitcast.30), calls=%async_computation.3 | async-start | bytes 524288 | tf_op jit(solution)/shard_map/all_to_all | solution.py:69
  101.5 8.7 %all-to-all-done.3 = f32[2,64,2,256]{3,2,0,1:T(2,128)S(1)} async-done(((f32[2,64,2,256]{3,2,0,1:T(2,128)}), f32[2,64,2,256]{3,2,0,1:T(2,128)S(1)}, u32[]{:S(2)}, u32[]{:S(2)}) %all-to-all-start.3) | async-done | bytes 262176 | tf_op jit(solution)/shard_map/all_to_all | solution.py:69
  110.5 0.9 pad_maximum_fusion.1
  (429 shorter events, 5.4 us)
Async XLA Ops:
  0.0 2.2 %copy-start = (f32[5,8,16,256]{3,2,1,0:T(8,128)S(1)}, f32[5,8,16,256]{3,2,1,0:T(8,128)}, u32[]{:S(2)}) copy-start(f32[5,8,16,256]{3,2,1,0:T(8,128)} %param.10) | copy-start | bytes 1966084
  2.4 19.7 %collective-permute-start = (f32[6,8,2,256]{3,1,2,0:T(8,128)S(1)}, f32[6,8,2,256]{3,1,2,0:T(8,128)S(1)}, u32[]{:S(2)}, u32[]{:S(2)}) collective-permute-start(f32[6,8,2,256]{3,1,2,0:T(8,128)S(1)} %copy.304), channel_id=1, source_target_pairs={{1,0},{2,1},{3,2},{4,3},{5,4},{6,5},{7,6},{8,7},{9,8},{10,9},{11,1... | collective-permute-start | bytes 294920 | tf_op jit(solution)/shard_map/ppermute | solution.py:18
  19.0 14.6 %collective-permute-start.1 = (f32[6,8,2,256]{3,1,2,0:T(8,128)S(1)}, f32[6,8,2,256]{3,1,2,0:T(8,128)S(1)}, u32[]{:S(2)}, u32[]{:S(2)}) collective-permute-start(f32[6,8,2,256]{3,1,2,0:T(8,128)S(1)} %copy.305), channel_id=1, source_target_pairs={{0,1},{1,2},{2,3},{3,4},{4,5},{5,6},{6,7},{7,8},{8,9},{9,10},{10,1... | collective-permute-start | bytes 294920 | tf_op jit(solution)/shard_map/ppermute | solution.py:15
  34.2 1.0 copy-start.2
  34.8 66.7 %copy-start.1 = (f32[5,8,16,256]{3,2,1,0:T(8,128)}, f32[5,8,16,256]{3,2,1,0:T(8,128)S(1)}, u32[]{:S(2)}) copy-start(f32[5,8,16,256]{3,2,1,0:T(8,128)S(1)} %fusion.195) | copy-start | bytes 1966084
  35.4 7.2 %copy-start.3 = (f32[4,8,16,256]{3,2,1,0:T(8,128)S(1)}, f32[4,8,16,256]{3,2,1,0:T(8,128)}, u32[]{:S(2)}) copy-start(f32[4,8,16,256]{3,2,1,0:T(8,128)} %param.14) | copy-start | bytes 1572868
  36.4 14.9 %all-to-all-start.2 = ((f32[2,8,16,256]{3,1,0,2:T(8,128)}), f32[2,8,16,256]{3,1,0,2:T(8,128)S(1)}, u32[]{:S(2)}, u32[]{:S(2)}) async-start(f32[2,8,16,256]{3,1,0,2:T(8,128)} %copy.287), calls=%async_computation.2 | async-start | bytes 524288 | tf_op jit(solution)/shard_map/all_to_all | solution.py:81
  42.6 13.1 %copy-start.4 = (f32[4,8,16,256]{3,2,1,0:T(8,128)S(1)}, f32[4,8,16,256]{3,2,1,0:T(8,128)}, u32[]{:S(2)}) copy-start(f32[4,8,16,256]{3,2,1,0:T(8,128)} %param.15) | copy-start | bytes 1572868
  51.3 18.8 %all-to-all-start.1 = ((f32[4,8,16,256]{3,1,0,2:T(8,128)}), f32[4,8,16,256]{3,1,0,2:T(8,128)S(1)}, u32[]{:S(2)}, u32[]{:S(2)}) async-start(f32[4,8,16,256]{3,1,0,2:T(8,128)} %copy.282), calls=%async_computation.1 | async-start | bytes 1048576 | tf_op jit(solution)/shard_map/all_to_all | solution.py:82
  70.2 18.8 %all-to-all-start = ((f32[4,8,16,256]{3,1,0,2:T(8,128)}), f32[4,8,16,256]{3,1,0,2:T(8,128)S(1)}, u32[]{:S(2)}, u32[]{:S(2)}) async-start(f32[4,8,16,256]{3,1,0,2:T(8,128)} %copy.279), calls=%async_computation | async-start | bytes 1048576 | tf_op jit(solution)/shard_map/all_to_all | solution.py:83
  97.2 13.0 %all-to-all-start.3 = ((f32[2,64,2,256]{3,2,0,1:T(2,128)}), f32[2,64,2,256]{3,2,0,1:T(2,128)S(1)}, u32[]{:S(2)}, u32[]{:S(2)}) async-start(f32[2,64,2,256]{3,2,0,1:T(2,128)} %bitcast.30), calls=%async_computation.3 | async-start | bytes 524288 | tf_op jit(solution)/shard_map/all_to_all | solution.py:69
  101.5 8.9 %slice-start = ((f32[5,8,16,256]{3,2,1,0:T(8,128)}), f32[2,8,16,256]{3,2,1,0:T(8,128)S(1)}, s32[]{:S(2)}) async-start(f32[5,8,16,256]{3,2,1,0:T(8,128)} %copy-done.1), calls=%async_computation.4 | async-start | bytes 524288 | tf_op jit(solution)/shard_map/slice | solution.py:86
where the time goes:
time: 112 us; the launch traced here: 111 us
  waiting for transfers between devices  50 us (45%)
  starting transfers between devices  37.8 us (34%)
  local copies, waits for them, and re-layouts  12.6 us (11%)
  other arithmetic  8.08 us (7%)
  loops' own time  2.67 us (2%)
    ppermute x1, starting transfers between devices, with_halo(): lax.ppermute(lax.slice_in_dim(block, 0, width, axis=dim), axis, backward)  16.6 us
    all_to_all x1, waiting for transfers between devices, local(): lax.all_to_all(lower_gain, 'lev', split_axis=2, concat_axis=1, tiled=True)  13.3 us
    ppermute x1, waiting for transfers between devices, with_halo(): lax.ppermute(lax.slice_in_dim(block, block.shape[dim] - width, None, axis...  11.5 us
    all_to_all x1, waiting for transfers between devices, local(): lax.all_to_all(upper_gain, 'lev', split_axis=2, concat_axis=1, tiled=True)  8.96 us
    all_to_all x1, waiting for transfers between devices, column_solve(): lax.all_to_all(solved, 'lev', split_axis=1, concat_axis=2, tiled=True)  8.69 us
    all_to_all x1, waiting for transfers between devices, local(): lax.all_to_all(forcing, 'lev', split_axis=2, concat_axis=1, tiled=True)  7.6 us
    all_to_all x1, starting transfers between devices, local(): lax.all_to_all(forcing, 'lev', split_axis=2, concat_axis=1, tiled=True)  6.24 us
    all_to_all x1, starting transfers between devices, local(): lax.all_to_all(lower_gain, 'lev', split_axis=2, concat_axis=1, tiled=True)  4.43 us
  transfers between devices with their start and end apart: 6, of which 5 were waited for; matrix products, arithmetic and copies ran while one was open for 7% of the time, Pallas kernels for 0%

commit v1 on v0

v1 whole, which is shorter than its diff:
```python
import functools

import jax
import jax.numpy as jnp
from jax import lax
from jax.experimental import pallas as pl
from jax.experimental.pallas import tpu as pltpu
from jax.sharding import PartitionSpec as P

MESH = pl.DeviceIdType.MESH
NEAR = 8.0 / 12.0
FAR = 1.0 / 12.0
TILE_ROWS = 8
TILE_LANES = 128
HALF = TILE_ROWS // 2


def difference(ahead_one, behind_one, ahead_two, behind_two):
    return NEAR * (ahead_one - behind_one) - FAR * (ahead_two - behind_two)


def rows_inside(values):
    count = values.shape[0]
    row = lax.broadcasted_iota(jnp.int32, values.shape, 0)
    return difference(
        jnp.where(row < count - 1, pltpu.roll(values, count - 1, 0), 0.0),
        jnp.where(row >= 1, pltpu.roll(values, 1, 0), 0.0),
        jnp.where(row < count - 2, pltpu.roll(values, count - 2, 0), 0.0),
        jnp.where(row >= 2, pltpu.roll(values, 2, 0), 0.0),
    )


def lanes_around(values):
    count = values.shape[1]
    return difference(
        pltpu.roll(values, count - 1, 1),
        pltpu.roll(values, 1, 1),
        pltpu.roll(values, count - 2, 1),
        pltpu.roll(values, 2, 1),
    )


def low_edge(row, two_below, one_below):
    return jnp.where(
        row == 0, FAR * two_below - NEAR * one_below, jnp.where(row == 1, FAR * one_below, 0.0)
    )


def high_edge(row, one_above, two_above):
    return jnp.where(
        row == TILE_ROWS - 1,
        NEAR * one_above - FAR * two_above,
        jnp.where(row == TILE_ROWS - 2, -FAR * one_above, 0.0),
    )


def times(left, right):
    return (
        left[0] * right[0] + left[1] * right[2],
        left[0] * right[1] + left[1] * right[3],
        left[2] * right[0] + left[3] * right[2],
        left[2] * right[1] + left[3] * right[3],
    )


def apply(matrix, vector):
    return (
        matrix[0] * vector[0] + matrix[1] * vector[1],
        matrix[2] * vector[0] + matrix[3] * vector[1],
    )


def plus(left, right):
    return tuple(a + b for a, b in zip(left, right))


def swapped(values):
    return pltpu.roll(values, HALF, 0)


def pack(upper, first, second):
    return (
        jnp.where(upper, first, swapped(second)),
        jnp.where(upper, swapped(first), second),
    )


def unpack(upper, low, high):
    return (
        jnp.where(upper, low, swapped(high)),
        jnp.where(upper, swapped(low), high),
    )


def kernel(
    levs,
    tiles,
    adjoint_hbm,
    courant_hbm,
    metric_hbm,
    pivot_hbm,
    lower_hbm,
    upper_hbm,
    out_hbm,
    adjoint,
    courant,
    metric,
    pivot,
    lower,
    upper,
    stepped,
    forcing,
    edge_send,
    edge_recv,
    side_send,
    side_recv,
    block_send,
    block_recv,
    carry_send,
    carry_recv,
    state_send,
    state_recv,
    load_sem,
    store_sem,
    edge_sems,
    side_sems,
    block_sems,
    carry_sems,
    state_sems,
):
    lev = lax.axis_index("lev")
    tile = lax.axis_index("tile")
    levels, rows, lanes = adjoint.shape[1:]
    right = lax.rem(tile + 1, tiles)
    left = lax.rem(tile + tiles - 1, tiles)

    def peer(offset):
        return lax.rem(lev + offset, levs)

    def slot_of(source):
        return lax.rem(lev + levs - source, levs)

    barrier = pltpu.get_barrier_semaphore()
    for target in (left, right):
        pl.semaphore_signal(barrier, inc=1, device_id=(lev, target), device_id_type=MESH)
    for offset in range(1, levs):
        pl.semaphore_signal(barrier, inc=1, device_id=(peer(offset), tile), device_id_type=MESH)

    loads = [
        pltpu.make_async_copy(source, target, load_sem.at[i])
        for i, (source, target) in enumerate(
            (
                (adjoint_hbm, adjoint),
                (courant_hbm, courant),
                (metric_hbm, metric),
                (lower_hbm, lower),
                (upper_hbm, upper),
                (pivot_hbm, pivot),
            )
        )
    ]
    for load in loads:
        load.start()
    for load in loads[:3]:
        load.wait()

    def critical(level, carry):
        drift = courant[0, level]
        side = courant[1, level]
        for place, field in ((0, 2), (1, 4)):
            here = adjoint[field, level]
            along = drift * here
            across = side * here
            if place:
                along = along + metric[0, level] * adjoint[0, level]
                across = across + metric[1, level] * adjoint[1, level]
            edge_send[0, place, level] = along[:2]
            edge_send[1, place, level] = along[rows - 2 :]
            stepped[field, level] = here + rows_inside(along) + lanes_around(across)
        return carry

    lax.fori_loop(0, levels, critical, 0)

    for load in loads[3:5]:
        load.wait()

    tile_shape = (TILE_ROWS, TILE_LANES)
    row = lax.broadcasted_iota(jnp.int32, tile_shape, 0)
    is_upper = row < HALF
    halves = lanes // TILE_LANES

    def part(index):
        return pl.ds(pl.multiple_of(index * TILE_LANES, TILE_LANES), TILE_LANES)

    def summarise(index, carry):
        for band in range(rows // TILE_ROWS):
            where = (pl.ds(band * TILE_ROWS, TILE_ROWS), part(index))

            def gain(ref, level):
                return tuple(ref[entry, level, where[0], where[1]] for entry in range(4))

            down = [gain(lower, 0)]
            for level in range(1, levels):
                down.append(times(gain(lower, level), down[-1]))
            up = gain(upper, levels - 1)
            mixed = down[-1]
            for level in range(levels - 2, -1, -1):
                step = gain(upper, level)
                mixed = plus(times(step, mixed), down[level])
                up = times(step, up)
            target = 2 * (band * halves + index)
            for place, matrix in enumerate((down[-1], up, mixed)):
                for kind, pair in enumerate(((matrix[0], matrix[3]), (matrix[1], matrix[2]))):
                    low, high = pack(is_upper, *pair)
                    block_send[target, 2 * place + kind] = low
                    block_send[target + 1, 2 * place + kind] = high
        return carry

    lax.fori_loop(0, halves, summarise, 0)

    pl.semaphore_wait(barrier, levs + 1)

    def to_sides(source, target, sems):
        copies = []
        for direction, where in ((0, left), (1, right)):
            copies.append(
                pltpu.make_async_remote_copy(
                    src_ref=source.at[direction],
                    dst_ref=target.at[direction],
                    send_sem=sems.at[0, direction],
                    recv_sem=sems.at[1, direction],
                    device_id=(lev, where),
                    device_id_type=MESH,
                )
            )
        for copy in copies:
            copy.start()
        return copies

    def to_levels(source, target, sems):
        copies = []
        for offset in range(1, levs):
            copies.append(
                pltpu.make_async_remote_copy(
                    src_ref=source.at[peer(offset)],
                    dst_ref=target.at[offset],
                    send_sem=sems.at[0, offset],
                    recv_sem=sems.at[1, offset],
                    device_id=(peer(offset), tile),
                    device_id_type=MESH,
                )
            )
        for copy in copies:
            copy.start()
        target[0] = source[lev]
        return copies

    edge_copies = to_sides(edge_send, edge_recv, edge_sems)
    block_copies = to_levels(block_send, block_recv, block_sems)

    def passive(level, carry):
        drift = courant[0, level]
        side = courant[1, level]
        for place, field in enumerate((0, 1, 3)):
            here = adjoint[field, level]
            along = drift * here
            side_send[0, place, level] = along[:2]
            side_send[1, place, level] = along[rows - 2 :]
            stepped[field, level] = here + rows_inside(along) + lanes_around(side * here)
        return carry

    lax.fori_loop(0, levels, passive, 0)
    side_copies = to_sides(side_send, side_recv, side_sems)

    loads[5].wait()
    for copy in edge_copies:
        copy.wait_recv()

    def correction(ref, place, level, band, lane_part):
        total = None
        if band == 0:
            total = low_edge(
                row,
                ref[1, place, level, pl.ds(0, 1), lane_part],
                ref[1, place, level, pl.ds(1, 1), lane_part],
            )
        if band == rows // TILE_ROWS - 1:
            high = high_edge(
                row,
                ref[0, place, level, pl.ds(0, 1), lane_part],
                ref[0, place, level, pl.ds(1, 1), lane_part],
            )
            total = high if total is None else total + high
        return total

    def force(index, carry):
        lane_part = part(index)
        for band in range(rows // TILE_ROWS):
            row_part = pl.ds(band * TILE_ROWS, TILE_ROWS)

            def gain(ref, level):
                return tuple(ref[entry, level, row_part, lane_part] for entry in range(4))

            falling = []
            for level in range(levels):
                pair = []
                for place, field in ((0, 2), (1, 4)):
                    value = stepped[field, level, row_part, lane_part]
                    fix = correction(edge_recv, place, level, band, lane_part)
                    pair.append(value if fix is None else value + fix)
                fresh = apply(gain(pivot, level), pair)
                for place in range(2):
                    forcing[place, level, row_part, lane_part] = fresh[place]
                if falling:
                    fresh = plus(apply(gain(lower, level), falling[-1]), fresh)
                falling.append(fresh)
            rising = falling[-1]
            for level in range(levels - 2, -1, -1):
                rising = plus(apply(gain(upper, level), rising), falling[level])
            target = 2 * (band * halves + index)
            for place, pair in enumerate((falling[-1], rising)):
                low, high = pack(is_upper, *pair)
                carry_send[target, place] = low
                carry_send[target + 1, place] = high
        return carry

    lax.fori_loop(0, halves, force, 0)
    carry_copies = to_levels(carry_send, carry_recv, carry_sems)

    for copy in block_copies:
        copy.wait_recv()
    for copy in carry_copies:
        copy.wait_recv()

    state = jnp.zeros(tile_shape, jnp.float32)
    states = []
    for block in range(levs):
        states.append(state)
        state_send[block, 0] = state
        if block < levs - 1:
            slot = slot_of(block)
            state = (
                block_recv[slot, 0] * state
                + block_recv[slot, 1] * swapped(state)
                + carry_recv[slot, 0]
            )
    state = jnp.zeros(tile_shape, jnp.float32)
    for block in range(levs - 1, -1, -1):
        state_send[block, 1] = state
        if block:
            slot = slot_of(block)
            state = (
                block_recv[slot, 2] * state
                + block_recv[slot, 3] * swapped(state)
                + block_recv[slot, 4] * states[block]
                + block_recv[slot, 5] * swapped(states[block])
                + carry_recv[slot, 1]
            )
    state_copies = to_levels(state_send, state_recv, state_sems)

    for copy in side_copies:
        copy.wait_recv()

    def finish(level, carry):
        lane_all = pl.ds(0, lanes)
        wide = lax.broadcasted_iota(jnp.int32, (TILE_ROWS, lanes), 0)
        for place, field in enumerate((0, 1, 3)):
            top = pl.ds(0, TILE_ROWS)
            bottom = pl.ds(rows - TILE_ROWS, TILE_ROWS)
            stepped[field, level, top] += low_edge(
                wide,
                side_recv[1, place, level, pl.ds(0, 1)],
                side_recv[1, place, level, pl.ds(1, 1)],
            )
            stepped[field, level, bottom] += high_edge(
                wide,
                side_recv[0, place, level, pl.ds(0, 1)],
                side_recv[0, place, level, pl.ds(1, 1)],
            )
        return carry

    lax.fori_loop(0, levels, finish, 0)

    stores = {
        field: pltpu.make_async_copy(stepped.at[field], out_hbm.at[field], store_sem.at[field])
        for field in range(5)
    }
    for field in (0, 1, 3):
        stores[field].start()

    for copy in state_copies:
        copy.wait_recv()

    def settle(index, carry):
        lane_part = part(index)
        for band in range(rows // TILE_ROWS):
            row_part = pl.ds(band * TILE_ROWS, TILE_ROWS)

            def gain(ref, level):
                return tuple(ref[entry, level, row_part, lane_part] for entry in range(4))

            source = 2 * (band * halves + index)
            low, high = slot_of(source), slot_of(source + 1)
            state = unpack(is_upper, state_recv[low, 0], state_recv[high, 0])
            falling = []
            for level in range(levels):
                fresh = tuple(forcing[place, level, row_part, lane_part] for place in range(2))
                state = plus(apply(gain(lower, level), state), fresh)
                falling.append(state)
            state = unpack(is_upper, state_recv[low, 1], state_recv[high, 1])
            for level in range(levels - 1, -1, -1):
                state = plus(apply(gain(upper, level), state), falling[level])
                stepped[2, level, row_part, lane_part] = state[0]
                stepped[4, level, row_part, lane_part] = state[1]
        return carry

    lax.fori_loop(0, halves, settle, 0)
    for field in (2, 4):
        stores[field].start()
    for copy in edge_copies + side_copies + block_copies + carry_copies + state_copies:
        copy.wait_send()
    for field in range(5):
        stores[field].wait()


def local(levs, tiles, adjoint, courant, metric, pivot_inverse, lower_gain, upper_gain):
    fields, levels, rows, lanes = adjoint.shape
    arrays = (adjoint, courant, metric, pivot_inverse, lower_gain, upper_gain)
    small = (TILE_ROWS, TILE_LANES)

    def vmem(*shape):
        return pltpu.VMEM(shape, jnp.float32)

    return pl.pallas_call(
        functools.partial(kernel, levs, tiles),
        out_shape=jax.ShapeDtypeStruct(adjoint.shape, jnp.float32),
        in_specs=[pl.BlockSpec(memory_space=pl.ANY)] * len(arrays),
        out_specs=pl.BlockSpec(memory_space=pl.ANY),
        scratch_shapes=[vmem(*array.shape) for array in arrays]
        + [
            vmem(*adjoint.shape),
            vmem(2, levels, rows, lanes),
            vmem(2, 2, levels, 2, lanes),
            vmem(2, 2, levels, 2, lanes),
            vmem(2, 3, levels, 2, lanes),
            vmem(2, 3, levels, 2, lanes),
            vmem(levs, 6, *small),
            vmem(levs, 6, *small),
            vmem(levs, 2, *small),
            vmem(levs, 2, *small),
            vmem(levs, 2, *small),
            vmem(levs, 2, *small),
            pltpu.SemaphoreType.DMA((len(arrays),)),
            pltpu.SemaphoreType.DMA((fields,)),
            pltpu.SemaphoreType.DMA((2, 2)),
            pltpu.SemaphoreType.DMA((2, 2)),
            pltpu.SemaphoreType.DMA((2, levs)),
            pltpu.SemaphoreType.DMA((2, levs)),
            pltpu.SemaphoreType.DMA((2, levs)),
        ],
        compiler_params=pltpu.CompilerParams(collective_id=0, has_side_effects=True),
    )(*arrays)


def solution(mesh):
    placed = P(None, "lev", "tile", None)
    return jax.shard_map(
        functools.partial(local, mesh.shape["lev"], mesh.shape["tile"]),
        mesh=mesh,
        in_specs=(placed,) * 6,
        out_specs=placed,
        check_vma=False,
    )
```

time: 112 us -> 33.6 us (0.30)
  waiting for transfers between devices: 50 us -> 0 us
  starting transfers between devices: 37.8 us -> 0 us
  Pallas kernels: 0 us -> 31.4 us
  local copies, waits for them, and re-layouts: 12.6 us -> 1.99 us
  other arithmetic: 8.08 us -> 0 us
  loops' own time: 2.67 us -> 0 us
    all_to_all x4 -> x0, waiting for transfers between devices: 38.5 us -> none  [the longest x1 13.3 us: local(): lax.all_to_all(lower_gain, 'lev', split_axis=2, concat_axis=1, tiled=True)]
    pallas_call x0 -> x1, Pallas kernels: none -> 31.4 us  [local(): pl.pallas_call(functools.partial(kernel, levs, tiles), out_shape=jax.Shap...]
    all_to_all x4 -> x0, starting transfers between devices: 19.3 us -> none  [the longest x1 6.24 us: local(): lax.all_to_all(forcing, 'lev', split_axis=2, concat_axis=1, tiled=True)]
    ppermute x2 -> x0, starting transfers between devices: 18.5 us -> none  [the longest x1 16.6 us: with_halo(): lax.ppermute(lax.slice_in_dim(block, 0, width, axis=dim), axis, backward)]
    ppermute x2 -> x0, waiting for transfers between devices: 11.5 us -> none  [the longest x1 11.5 us: with_halo(): lax.ppermute(lax.slice_in_dim(block, block.shape[dim] - width, None, axis...]
    slice x23 -> x0, local copies, waits for them, and re-layouts: 3.98 us -> none  [the longest x8 2.58 us: mat_vec(): system_matrix[0] * vector[0] + system_matrix[1] * vector[1]]
    add x258 -> x0, other arithmetic: 3.23 us -> none  [the longest x129 1.33 us: mat_vec(): system_matrix[0] * vector[0] + system_matrix[1] * vector[1]]
    another operation x2 -> x0, loops' own time: 2.67 us -> none  [chain_run(): lax.scan(advance, initial, (jnp.moveaxis(coupling, 1, 0), jnp.moveaxis(fo...]
  transfers between devices with their start and end apart: 6 -> 0, of which waited for: 5 -> 0; matrix products, arithmetic and copies ran while one was open for 7% -> 0% of each run, Pallas kernels for 0% -> 0%
where the time goes in v1:
time: 33.6 us; the launch traced here: 33.4 us
  Pallas kernels  31.4 us (93%)
  local copies, waits for them, and re-layouts  1.99 us (6%)
    pallas_call x1, Pallas kernels, local(): pl.pallas_call(functools.partial(kernel, levs, tiles), out_shape=jax.Shap...  31.4 us
    unnamed x1, local copies, waits for them, and re-layouts  1.99 us

profile of v1, /device:TPU:1, one launch (start us, length us, event | category | flops | bytes accessed | tf_op | source)
XLA Modules:
  0.0 33.4 jit_solution(18389419021850786918)
XLA Ops:
  0.0 31.4 %shard_map.64 = f32[5,8,16,256]{3,2,1,0:T(8,128)} custom-call(f32[5,8,16,256]{3,2,1,0:T(8,128)} %adjoint_hbm.1, f32[2,8,16,256]{3,2,1,0:T(8,128)} %courant_hbm.1, f32[2,8,16,256]{3,2,1,0:T(8,128)} %metric_hbm.1, f32[4,8,16,256]{3,2,1,0:T(8,128)} %pivot_hbm.1, f32[4,8,16,256]{3,2,1,0:T(8,128)} %lower_hbm.1, f32[4,8,16,256]{3,2,1,0:T(8,128)} %upper_hbm.1), custom_call_target="tpu_custom_call" | custom-call | tf_op jit(solution)/shard_map/pallas_call | solution.py:434
  31.4 2.0 %copy.8 = f32[5,8,16,256]{3,2,1,0:T(8,128)} copy(f32[5,8,16,256]{3,2,1,0:T(8,128)} %shard_map.64) | data formatting | bytes 1310720

commit v2 on v1

v2 whole, which is shorter than its diff:
```python
import functools

import jax
import jax.numpy as jnp
from jax import lax
from jax.experimental import pallas as pl
from jax.experimental.pallas import tpu as pltpu
from jax.sharding import PartitionSpec as P

MESH = pl.DeviceIdType.MESH
NEAR = 8.0 / 12.0
FAR = 1.0 / 12.0
TILE_ROWS = 8
TILE_LANES = 128


def difference(ahead_one, behind_one, ahead_two, behind_two):
    return NEAR * (ahead_one - behind_one) - FAR * (ahead_two - behind_two)


def rows_inside(values):
    count = values.shape[0]
    row = lax.broadcasted_iota(jnp.int32, values.shape, 0)
    return difference(
        jnp.where(row < count - 1, pltpu.roll(values, count - 1, 0), 0.0),
        jnp.where(row >= 1, pltpu.roll(values, 1, 0), 0.0),
        jnp.where(row < count - 2, pltpu.roll(values, count - 2, 0), 0.0),
        jnp.where(row >= 2, pltpu.roll(values, 2, 0), 0.0),
    )


def lanes_around(values):
    count = values.shape[1]
    return difference(
        pltpu.roll(values, count - 1, 1),
        pltpu.roll(values, 1, 1),
        pltpu.roll(values, count - 2, 1),
        pltpu.roll(values, 2, 1),
    )


def low_edge(row, two_below, one_below):
    return jnp.where(
        row == 0, FAR * two_below - NEAR * one_below, jnp.where(row == 1, FAR * one_below, 0.0)
    )


def high_edge(row, one_above, two_above):
    return jnp.where(
        row == TILE_ROWS - 1,
        NEAR * one_above - FAR * two_above,
        jnp.where(row == TILE_ROWS - 2, -FAR * one_above, 0.0),
    )


def times(left, right):
    return (
        left[0] * right[0] + left[1] * right[2],
        left[0] * right[1] + left[1] * right[3],
        left[2] * right[0] + left[3] * right[2],
        left[2] * right[1] + left[3] * right[3],
    )


def apply(matrix, vector):
    return (
        matrix[0] * vector[0] + matrix[1] * vector[1],
        matrix[2] * vector[0] + matrix[3] * vector[1],
    )


def plus(left, right):
    return tuple(a + b for a, b in zip(left, right))


def kernel(
    levs,
    tiles,
    adjoint_hbm,
    courant_hbm,
    metric_hbm,
    pivot_hbm,
    lower_hbm,
    upper_hbm,
    stepped,
    adjoint,
    courant,
    metric,
    pivot,
    lower,
    upper,
    forcing,
    edge_send,
    edge_recv,
    side_send,
    side_recv,
    block_send,
    block_recv,
    carry_send,
    carry_recv,
    state_send,
    state_recv,
    load_sem,
    edge_sems,
    side_sems,
    block_sems,
    carry_sems,
    state_sems,
):
    lev = lax.axis_index("lev")
    tile = lax.axis_index("tile")
    levels, rows, lanes = adjoint.shape[1:]
    right = lax.rem(tile + 1, tiles)
    left = lax.rem(tile + tiles - 1, tiles)

    def peer(offset):
        return lax.rem(lev + offset, levs)

    def slot_of(source):
        return lax.rem(lev + levs - source, levs)

    parts = block_send.shape[0]
    first = (levs - parts) // 2

    def solves(device):
        return jnp.logical_and(device >= first, device < first + parts)

    solver = solves(lev)

    barrier = pltpu.get_barrier_semaphore()
    for target in (left, right):
        pl.semaphore_signal(barrier, inc=1, device_id=(lev, target), device_id_type=MESH)
    for offset in range(1, levs):

        @pl.when(jnp.logical_or(solver, solves(peer(offset))))
        def _():
            pl.semaphore_signal(barrier, inc=1, device_id=(peer(offset), tile), device_id_type=MESH)

    order = (
        [(adjoint_hbm.at[field], adjoint.at[field]) for field in (0, 2, 4)]
        + [(courant_hbm.at[0], courant.at[0]), (metric_hbm.at[0], metric.at[0])]
        + [(lower_hbm, lower), (upper_hbm, upper)]
        + [(courant_hbm.at[1], courant.at[1]), (metric_hbm.at[1], metric.at[1])]
        + [(adjoint_hbm.at[field], adjoint.at[field]) for field in (1, 3)]
        + [(pivot_hbm, pivot)]
    )
    loads = [
        pltpu.make_async_copy(source, target, load_sem.at[i])
        for i, (source, target) in enumerate(order)
    ]
    for load in loads:
        load.start()
    for load in loads[:5]:
        load.wait()

    def weighted(level, field):
        along = courant[0, level] * adjoint[field, level]
        if field == 4:
            along = along + metric[0, level] * adjoint[0, level]
        return along

    def edges(level, carry):
        for place, field in ((0, 2), (1, 4)):
            along = weighted(level, field)
            edge_send[0, place, level] = along[:2]
            edge_send[1, place, level] = along[rows - 2 :]
        return carry

    lax.fori_loop(0, levels, edges, 0)

    @pl.when(solver)
    def _():
        pl.semaphore_wait(barrier, levs + 1)

    @pl.when(jnp.logical_not(solver))
    def _():
        pl.semaphore_wait(barrier, parts + 2)

    def to_sides(source, target, sems):
        copies = []
        for direction, where in ((0, left), (1, right)):
            copies.append(
                pltpu.make_async_remote_copy(
                    src_ref=source.at[direction],
                    dst_ref=target.at[direction],
                    send_sem=sems.at[0, direction],
                    recv_sem=sems.at[1, direction],
                    device_id=(lev, where),
                    device_id_type=MESH,
                )
            )
        for copy in copies:
            copy.start()
        return copies

    def level_copy(source, target, sems, offset, place):
        return pltpu.make_async_remote_copy(
            src_ref=source.at[place],
            dst_ref=target.at[offset],
            send_sem=sems.at[0, offset],
            recv_sem=sems.at[1, offset],
            device_id=(peer(offset), tile),
            device_id_type=MESH,
        )

    def part_of(device):
        return jnp.clip(device - first, 0, parts - 1)

    def to_solvers(source, target, sems, starting):
        for offset in range(1, levs):

            @pl.when(solves(peer(offset)))
            def _():
                copy = level_copy(source, target, sems, offset, part_of(peer(offset)))
                if starting:
                    copy.start()
                else:
                    copy.wait_send()

    def at_solver(source, target, sems):
        target[0] = source[part_of(lev)]
        for offset in range(1, levs):
            level_copy(source, target, sems, offset, 0).wait_recv()

    edge_copies = to_sides(edge_send, edge_recv, edge_sems)

    for load in loads[5:7]:
        load.wait()

    tile_shape = (TILE_ROWS, TILE_LANES)
    row = lax.broadcasted_iota(jnp.int32, tile_shape, 0)
    halves = lanes // TILE_LANES

    def part(index):
        return pl.ds(pl.multiple_of(index * TILE_LANES, TILE_LANES), TILE_LANES)

    def summarise(index, carry):
        for band in range(rows // TILE_ROWS):
            where = (pl.ds(band * TILE_ROWS, TILE_ROWS), part(index))

            def gain(ref, level):
                return tuple(ref[entry, level, where[0], where[1]] for entry in range(4))

            down = [gain(lower, 0)]
            for level in range(1, levels):
                down.append(times(gain(lower, level), down[-1]))
            up = gain(upper, levels - 1)
            mixed = down[-1]
            for level in range(levels - 2, -1, -1):
                step = gain(upper, level)
                mixed = plus(times(step, mixed), down[level])
                up = times(step, up)
            target = band * halves + index
            for place, matrix in enumerate((down[-1], up, mixed)):
                for entry in range(4):
                    block_send[target, 4 * place + entry] = matrix[entry]
        return carry

    lax.fori_loop(0, halves, summarise, 0)

    to_solvers(block_send, block_recv, block_sems, True)

    for load in loads[7:]:
        load.wait()

    def critical(level, carry):
        for field in (2, 4):
            here = adjoint[field, level]
            across = courant[1, level] * here
            if field == 4:
                across = across + metric[1, level] * adjoint[1, level]
            along = rows_inside(weighted(level, field))
            stepped[field, level] = here + along + lanes_around(across)
        return carry

    lax.fori_loop(0, levels, critical, 0)

    def passive(level, carry):
        drift = courant[0, level]
        side = courant[1, level]
        for place, field in enumerate((0, 1, 3)):
            here = adjoint[field, level]
            along = drift * here
            side_send[0, place, level] = along[:2]
            side_send[1, place, level] = along[rows - 2 :]
            stepped[field, level] = here + rows_inside(along) + lanes_around(side * here)
        return carry

    lax.fori_loop(0, levels, passive, 0)
    side_copies = to_sides(side_send, side_recv, side_sems)

    for copy in edge_copies:
        copy.wait_recv()

    def correction(ref, place, level, band, lane_part):
        total = None
        if band == 0:
            total = low_edge(
                row,
                ref[1, place, level, pl.ds(0, 1), lane_part],
                ref[1, place, level, pl.ds(1, 1), lane_part],
            )
        if band == rows // TILE_ROWS - 1:
            high = high_edge(
                row,
                ref[0, place, level, pl.ds(0, 1), lane_part],
                ref[0, place, level, pl.ds(1, 1), lane_part],
            )
            total = high if total is None else total + high
        return total

    def force(index, carry):
        lane_part = part(index)
        for band in range(rows // TILE_ROWS):
            row_part = pl.ds(band * TILE_ROWS, TILE_ROWS)

            def gain(ref, level):
                return tuple(ref[entry, level, row_part, lane_part] for entry in range(4))

            falling = []
            for level in range(levels):
                pair = []
                for place, field in ((0, 2), (1, 4)):
                    value = stepped[field, level, row_part, lane_part]
                    fix = correction(edge_recv, place, level, band, lane_part)
                    pair.append(value if fix is None else value + fix)
                fresh = apply(gain(pivot, level), pair)
                for place in range(2):
                    forcing[place, level, row_part, lane_part] = fresh[place]
                if falling:
                    fresh = plus(apply(gain(lower, level), falling[-1]), fresh)
                falling.append(fresh)
            rising = falling[-1]
            for level in range(levels - 2, -1, -1):
                rising = plus(apply(gain(upper, level), rising), falling[level])
            target = band * halves + index
            for place, value in enumerate(falling[-1] + rising):
                carry_send[target, place] = value
        return carry

    lax.fori_loop(0, halves, force, 0)
    to_solvers(carry_send, carry_recv, carry_sems, True)

    @pl.when(solver)
    def _():
        at_solver(block_send, block_recv, block_sems)
        at_solver(carry_send, carry_recv, carry_sems)

        def matrix(slot, place):
            return tuple(block_recv[slot, 4 * place + entry] for entry in range(4))

        def vector(slot, place):
            return tuple(carry_recv[slot, 2 * place + entry] for entry in range(2))

        nothing = jnp.zeros(tile_shape, jnp.float32)
        state = (nothing, nothing)
        states = []
        for block in range(levs):
            states.append(state)
            for entry in range(2):
                state_send[block, entry] = state[entry]
            if block < levs - 1:
                slot = slot_of(block)
                state = plus(apply(matrix(slot, 0), state), vector(slot, 0))
        state = (nothing, nothing)
        for block in range(levs - 1, -1, -1):
            for entry in range(2):
                state_send[block, 2 + entry] = state[entry]
            if block:
                slot = slot_of(block)
                state = plus(
                    apply(matrix(slot, 1), state),
                    plus(apply(matrix(slot, 2), states[block]), vector(slot, 1)),
                )
        for offset in range(1, levs):
            level_copy(state_send, state_recv, state_sems, offset, peer(offset)).start()
        state_recv[0] = state_send[lev]

    for copy in side_copies:
        copy.wait_recv()

    def finish(level, carry):
        wide = lax.broadcasted_iota(jnp.int32, (TILE_ROWS, lanes), 0)
        for place, field in enumerate((0, 1, 3)):
            top = pl.ds(0, TILE_ROWS)
            bottom = pl.ds(rows - TILE_ROWS, TILE_ROWS)
            stepped[field, level, top] += low_edge(
                wide,
                side_recv[1, place, level, pl.ds(0, 1)],
                side_recv[1, place, level, pl.ds(1, 1)],
            )
            stepped[field, level, bottom] += high_edge(
                wide,
                side_recv[0, place, level, pl.ds(0, 1)],
                side_recv[0, place, level, pl.ds(1, 1)],
            )
        return carry

    lax.fori_loop(0, levels, finish, 0)

    for offset in range(1, levs):

        @pl.when(solves(lax.rem(lev + levs - offset, levs)))
        def _():
            level_copy(state_send, state_recv, state_sems, offset, 0).wait_recv()

    def settle(index, carry):
        lane_part = part(index)
        for band in range(rows // TILE_ROWS):
            row_part = pl.ds(band * TILE_ROWS, TILE_ROWS)

            def gain(ref, level):
                return tuple(ref[entry, level, row_part, lane_part] for entry in range(4))

            slot = slot_of(first + band * halves + index)
            state = (state_recv[slot, 0], state_recv[slot, 1])
            falling = []
            for level in range(levels):
                fresh = tuple(forcing[place, level, row_part, lane_part] for place in range(2))
                state = plus(apply(gain(lower, level), state), fresh)
                falling.append(state)
            state = (state_recv[slot, 2], state_recv[slot, 3])
            for level in range(levels - 1, -1, -1):
                state = plus(apply(gain(upper, level), state), falling[level])
                stepped[2, level, row_part, lane_part] = state[0]
                stepped[4, level, row_part, lane_part] = state[1]
        return carry

    lax.fori_loop(0, halves, settle, 0)
    for copy in edge_copies + side_copies:
        copy.wait_send()
    to_solvers(block_send, block_recv, block_sems, False)
    to_solvers(carry_send, carry_recv, carry_sems, False)

    @pl.when(solver)
    def _():
        for offset in range(1, levs):
            level_copy(state_send, state_recv, state_sems, offset, 0).wait_send()


def local(levs, tiles, adjoint, courant, metric, pivot_inverse, lower_gain, upper_gain):
    fields, levels, rows, lanes = adjoint.shape
    arrays = (adjoint, courant, metric, pivot_inverse, lower_gain, upper_gain)
    small = (TILE_ROWS, TILE_LANES)
    parts = rows * lanes // (TILE_ROWS * TILE_LANES)

    def vmem(*shape):
        return pltpu.VMEM(shape, jnp.float32)

    return pl.pallas_call(
        functools.partial(kernel, levs, tiles),
        out_shape=pltpu.VMEM(adjoint.shape, jnp.float32),
        in_specs=[pl.BlockSpec(memory_space=pl.ANY)] * len(arrays),
        out_specs=pl.BlockSpec(memory_space=pltpu.VMEM),
        scratch_shapes=[vmem(*array.shape) for array in arrays]
        + [
            vmem(2, levels, rows, lanes),
            vmem(2, 2, levels, 2, lanes),
            vmem(2, 2, levels, 2, lanes),
            vmem(2, 3, levels, 2, lanes),
            vmem(2, 3, levels, 2, lanes),
            vmem(parts, 12, *small),
            vmem(levs, 12, *small),
            vmem(parts, 4, *small),
            vmem(levs, 4, *small),
            vmem(levs, 4, *small),
            vmem(levs, 4, *small),
            pltpu.SemaphoreType.DMA((12,)),
            pltpu.SemaphoreType.DMA((2, 2)),
            pltpu.SemaphoreType.DMA((2, 2)),
            pltpu.SemaphoreType.DMA((2, levs)),
            pltpu.SemaphoreType.DMA((2, levs)),
            pltpu.SemaphoreType.DMA((2, levs)),
        ],
        compiler_params=pltpu.CompilerParams(collective_id=0, has_side_effects=True),
    )(*arrays)


def solution(mesh):
    placed = P(None, "lev", "tile", None)
    return jax.shard_map(
        functools.partial(local, mesh.shape["lev"], mesh.shape["tile"]),
        mesh=mesh,
        in_specs=(placed,) * 6,
        out_specs=placed,
        check_vma=False,
    )
```

time: 33.6 us -> 29.6 us (0.88)
  Pallas kernels: 31.4 us -> 28.6 us
  local copies, waits for them, and re-layouts: 1.99 us -> 0.84 us
    pallas_call x1, Pallas kernels: 31.4 us -> 28.6 us  [local(): pl.pallas_call(functools.partial(kernel, levs, tiles), out_shape=pltpu.VM...]
    unnamed x1, local copies, waits for them, and re-layouts: 1.99 us -> 0.84 us
where the time goes in v2:
time: 29.6 us; the launch traced here: 29.5 us
  Pallas kernels  28.6 us (97%)
  local copies, waits for them, and re-layouts  0.84 us (3%)
    pallas_call x1, Pallas kernels, local(): pl.pallas_call(functools.partial(kernel, levs, tiles), out_shape=pltpu.VM...  28.6 us
    unnamed x1, local copies, waits for them, and re-layouts  0.84 us

profile of v2, /device:TPU:1, one launch (start us, length us, event | category | flops | bytes accessed | tf_op | source)
XLA Modules:
  0.0 29.5 jit_solution(17623229410008214805)
XLA Ops:
  0.0 28.6 %shard_map.64 = f32[5,8,16,256]{3,2,1,0:T(8,128)S(1)} custom-call(f32[5,8,16,256]{3,2,1,0:T(8,128)} %adjoint_hbm.1, f32[2,8,16,256]{3,2,1,0:T(8,128)} %courant_hbm.1, f32[2,8,16,256]{3,2,1,0:T(8,128)} %metric_hbm.1, f32[4,8,16,256]{3,2,1,0:T(8,128)} %pivot_hbm.1, f32[4,8,16,256]{3,2,1,0:T(8,128)} %lower_hbm.1, f32[4,8,16,256]{3,2,1,0:T(8,128)} %upper_hbm.1), custom_call_target="tpu_custom_call" | custom-call | tf_op jit(solution)/shard_map/pallas_call | solution.py:450
  28.6 0.8 %copy.8 = f32[5,8,16,256]{3,2,1,0:T(8,128)} copy(f32[5,8,16,256]{3,2,1,0:T(8,128)S(1)} %shard_map.64) | data formatting | bytes 1310720

commit v3 on v2

--- a/solution.py
+++ b/solution.py
@@ -90,6 +90,8 @@
     lower,
     upper,
     forcing,
+    narrow_gain,
+    narrow_forcing,
     edge_send,
     edge_recv,
     side_send,
@@ -100,12 +102,22 @@
     carry_recv,
     state_send,
     state_recv,
+    edge_block_send,
+    edge_block_recv,
+    extra_send,
+    extra_recv,
+    tail_send,
+    tail_recv,
     load_sem,
     edge_sems,
     side_sems,
     block_sems,
     carry_sems,
     state_sems,
+    edge_block_sems,
+    extra_sems,
+    tail_sems,
+    open_sem,
 ):
     lev = lax.axis_index("lev")
     tile = lax.axis_index("tile")
@@ -127,14 +139,23 @@
 
     solver = solves(lev)
 
+    chief = 1
+
+    opener = tile == 0
+    answerer = tile == tiles - 1
+
     barrier = pltpu.get_barrier_semaphore()
-    for target in (left, right):
-        pl.semaphore_signal(barrier, inc=1, device_id=(lev, target), device_id_type=MESH)
+    for target, is_long in ((left, opener), (right, answerer)):
+
+        @pl.when(jnp.logical_not(is_long))
+        def _():
+            pl.semaphore_signal(barrier, inc=1, device_id=(lev, target), device_id_type=MESH)
+
     for offset in range(1, levs):
-
-        @pl.when(jnp.logical_or(solver, solves(peer(offset))))
-        def _():
-            pl.semaphore_signal(barrier, inc=1, device_id=(peer(offset), tile), device_id_type=MESH)
+        pl.semaphore_signal(barrier, inc=1, device_id=(peer(offset), tile), device_id_type=MESH)
+
+    halves = lanes // TILE_LANES
+    bands = rows // TILE_ROWS
 
     order = (
         [(adjoint_hbm.at[field], adjoint.at[field]) for field in (0, 2, 4)]
@@ -148,10 +169,12 @@
         pltpu.make_async_copy(source, target, load_sem.at[i])
         for i, (source, target) in enumerate(order)
     ]
-    for load in loads:
+    for load in loads[:5]:
         load.start()
     for load in loads[:5]:
         load.wait()
+    for load in loads[5:]:
+        load.start()
 
     def weighted(level, field):
         along = courant[0, level] * adjoint[field, level]
@@ -162,40 +185,60 @@
     def edges(level, carry):
         for place, field in ((0, 2), (1, 4)):
             along = weighted(level, field)
-            edge_send[0, place, level] = along[:2]
-            edge_send[1, place, level] = along[rows - 2 :]
-        return carry
-
-    lax.fori_loop(0, levels, edges, 0)
-
-    @pl.when(solver)
+            ends = [along[i : i + 1] for i in (0, 1, rows - 2, rows - 1)]
+            sent = (
+                (-FAR * ends[0], NEAR * ends[0] - FAR * ends[1]),
+                (FAR * ends[2] - NEAR * ends[3], FAR * ends[3]),
+            )
+            for direction in range(2):
+                for half in range(halves):
+                    for i in range(2):
+                        edge_send[direction, place, level, 2 * half + i : 2 * half + i + 1] = sent[
+                            direction
+                        ][i][:, half * TILE_LANES : (half + 1) * TILE_LANES]
+        return carry
+
+    lax.fori_loop(0, levels, edges, 0, unroll=True)
+
+    @pl.when(jnp.logical_not(opener))
     def _():
         pl.semaphore_wait(barrier, levs + 1)
 
-    @pl.when(jnp.logical_not(solver))
-    def _():
-        pl.semaphore_wait(barrier, parts + 2)
+    @pl.when(opener)
+    def _():
+        pl.semaphore_wait(barrier, levs)
+
+    @pl.when(opener)
+    def _():
+        pl.semaphore_signal(barrier, inc=1, device_id=(lev, tiles - 1), device_id_type=MESH)
+
+    @pl.when(answerer)
+    def _():
+        pl.semaphore_signal(open_sem, inc=1, device_id=(lev, 0), device_id_type=MESH)
+
+    sides = (left, right)
+
+    def to_side(source, target, sems, direction):
+        return pltpu.make_async_remote_copy(
+            src_ref=source.at[direction],
+            dst_ref=target.at[direction],
+            send_sem=sems.at[0, direction],
+            recv_sem=sems.at[1, direction],
+            device_id=(lev, sides[direction]),
+            device_id_type=MESH,
+        )
 
     def to_sides(source, target, sems):
-        copies = []
-        for direction, where in ((0, left), (1, right)):
-            copies.append(
-                pltpu.make_async_remote_copy(
-                    src_ref=source.at[direction],
-                    dst_ref=target.at[direction],
-                    send_sem=sems.at[0, direction],
-                    recv_sem=sems.at[1, direction],
-                    device_id=(lev, where),
-                    device_id_type=MESH,
-                )
-            )
-        for copy in copies:
-            copy.start()
-        return copies
+        @pl.when(jnp.logical_not(opener))
+        def _():
+            to_side(source, target, sems, 0).start()
+
+        to_side(source, target, sems, 1).start()
+        return [to_side(source, target, sems, direction) for direction in range(2)]
 
     def level_copy(source, target, sems, offset, place):
         return pltpu.make_async_remote_copy(
-            src_ref=source.at[place],
+            src_ref=source if place is None else source.at[place],
             dst_ref=target.at[offset],
             send_sem=sems.at[0, offset],
             recv_sem=sems.at[1, offset],
@@ -217,6 +260,22 @@
                 else:
                     copy.wait_send()
 
+    def to_chief(source, target, sems, starting):
+        for offset in range(1, levs):
+
+            @pl.when(peer(offset) == chief)
+            def _():
+                copy = level_copy(source, target, sems, offset, None)
+                if starting:
+                    copy.start()
+                else:
+                    copy.wait_send()
+
+    def at_chief(source, target, sems):
+        target[0] = source[...]
+        for offset in range(1, levs):
+            level_copy(target.at[0], target, sems, offset, None).wait_recv()
+
     def at_solver(source, target, sems):
         target[0] = source[part_of(lev)]
         for offset in range(1, levs):
@@ -229,13 +288,12 @@
 
     tile_shape = (TILE_ROWS, TILE_LANES)
     row = lax.broadcasted_iota(jnp.int32, tile_shape, 0)
-    halves = lanes // TILE_LANES
 
     def part(index):
         return pl.ds(pl.multiple_of(index * TILE_LANES, TILE_LANES), TILE_LANES)
 
     def summarise(index, carry):
-        for band in range(rows // TILE_ROWS):
+        for band in range(bands):
             where = (pl.ds(band * TILE_ROWS, TILE_ROWS), part(index))
 
             def gain(ref, level):
@@ -257,8 +315,8 @@
         return carry
 
     lax.fori_loop(0, halves, summarise, 0)
-
     to_solvers(block_send, block_recv, block_sems, True)
+
 
     for load in loads[7:]:
         load.wait()
@@ -275,43 +333,9 @@
 
     lax.fori_loop(0, levels, critical, 0)
 
-    def passive(level, carry):
-        drift = courant[0, level]
-        side = courant[1, level]
-        for place, field in enumerate((0, 1, 3)):
-            here = adjoint[field, level]
-            along = drift * here
-            side_send[0, place, level] = along[:2]
-            side_send[1, place, level] = along[rows - 2 :]
-            stepped[field, level] = here + rows_inside(along) + lanes_around(side * here)
-        return carry
-
-    lax.fori_loop(0, levels, passive, 0)
-    side_copies = to_sides(side_send, side_recv, side_sems)
-
-    for copy in edge_copies:
-        copy.wait_recv()
-
-    def correction(ref, place, level, band, lane_part):
-        total = None
-        if band == 0:
-            total = low_edge(
-                row,
-                ref[1, place, level, pl.ds(0, 1), lane_part],
-                ref[1, place, level, pl.ds(1, 1), lane_part],
-            )
-        if band == rows // TILE_ROWS - 1:
-            high = high_edge(
-                row,
-                ref[0, place, level, pl.ds(0, 1), lane_part],
-                ref[0, place, level, pl.ds(1, 1), lane_part],
-            )
-            total = high if total is None else total + high
-        return total
-
     def force(index, carry):
         lane_part = part(index)
-        for band in range(rows // TILE_ROWS):
+        for band in range(bands):
             row_part = pl.ds(band * TILE_ROWS, TILE_ROWS)
 
             def gain(ref, level):
@@ -319,11 +343,7 @@
 
             falling = []
             for level in range(levels):
-                pair = []
-                for place, field in ((0, 2), (1, 4)):
-                    value = stepped[field, level, row_part, lane_part]
-                    fix = correction(edge_recv, place, level, band, lane_part)
-                    pair.append(value if fix is None else value + fix)
+                pair = tuple(stepped[field, level, row_part, lane_part] for field in (2, 4))
                 fresh = apply(gain(pivot, level), pair)
                 for place in range(2):
                     forcing[place, level, row_part, lane_part] = fresh[place]
@@ -341,40 +361,139 @@
     lax.fori_loop(0, halves, force, 0)
     to_solvers(carry_send, carry_recv, carry_sems, True)
 
-    @pl.when(solver)
-    def _():
-        at_solver(block_send, block_recv, block_sems)
-        at_solver(carry_send, carry_recv, carry_sems)
-
+    def passive(level, carry):
+        drift = courant[0, level]
+        side = courant[1, level]
+        for place, field in enumerate((0, 1, 3)):
+            here = adjoint[field, level]
+            along = drift * here
+            side_send[0, place, level] = along[:2]
+            side_send[1, place, level] = along[rows - 2 :]
+            stepped[field, level] = here + rows_inside(along) + lanes_around(side * here)
+        return carry
+
+    lax.fori_loop(0, levels, passive, 0)
+
+    def turned(values, pairs):
+        shift = 2 * (pairs % parts)
+        return pltpu.roll(values, shift, 0) if shift else values
+
+    def at_pair(pair):
+        return jnp.logical_and(row >= 2 * pair, row < 2 * pair + 2)
+
+    def home(index):
+        return (parts - 1) * (index // halves)
+
+    def ends_of(load):
+        total = None
+        for index in range(parts):
+            band, half = divmod(index, halves)
+            values = load(
+                pl.ds(band * TILE_ROWS, TILE_ROWS), pl.ds(half * TILE_LANES, TILE_LANES)
+            )
+            values = turned(values, index - home(index))
+            total = values if total is None else jnp.where(at_pair(index), values, total)
+        return total
+
+    def narrow(level, carry):
+        for place, ref in enumerate((pivot, lower, upper)):
+            for entry in range(4):
+                narrow_gain[place, entry, level] = ends_of(
+                    lambda row_part, lane_part: ref[entry, level, row_part, lane_part]
+                )
+        for place in range(2):
+            narrow_forcing[place, level] = ends_of(
+                lambda row_part, lane_part: forcing[place, level, row_part, lane_part]
+            )
+        return carry
+
+    lax.fori_loop(0, levels, narrow, 0)
+
+    for entry in range(12):
+        total = None
+        for index in range(parts):
+            values = turned(block_send[index, entry], index - home(index))
+            total = values if total is None else jnp.where(at_pair(index), values, total)
+        edge_block_send[entry] = total
+    to_chief(edge_block_send, edge_block_recv, edge_block_sems, True)
+    side_copies = to_sides(side_send, side_recv, side_sems)
+
+    def narrow_matrix(place, level):
+        return tuple(narrow_gain[place, entry, level] for entry in range(4))
+
+    def mend():
+        for copy in edge_copies:
+            copy.wait_recv()
+        falling = []
+        for level in range(levels):
+            pair = tuple(
+                jnp.concatenate([edge_recv[1, place, level], edge_recv[0, place, level]], axis=0)
+                for place in range(2)
+            )
+            fresh = apply(narrow_matrix(0, level), pair)
+            fresh = plus(tuple(narrow_forcing[place, level] for place in range(2)), fresh)
+            for place in range(2):
+                narrow_forcing[place, level] = fresh[place]
+            if falling:
+                fresh = plus(apply(narrow_matrix(1, level), falling[-1]), fresh)
+            falling.append(fresh)
+        rising = falling[-1]
+        for level in range(levels - 2, -1, -1):
+            rising = plus(apply(narrow_matrix(2, level), rising), falling[level])
+        for place, value in enumerate(falling[-1] + rising):
+            extra_send[place] = value
+        to_chief(extra_send, extra_recv, extra_sems, True)
+
+    pl.when(jnp.logical_not(opener))(mend)
+
+    def solve(maps, vectors, target):
         def matrix(slot, place):
-            return tuple(block_recv[slot, 4 * place + entry] for entry in range(4))
+            return tuple(maps[slot, 4 * place + entry] for entry in range(4))
 
         def vector(slot, place):
-            return tuple(carry_recv[slot, 2 * place + entry] for entry in range(2))
+            return tuple(vectors[slot, 2 * place + entry] for entry in range(2))
 
         nothing = jnp.zeros(tile_shape, jnp.float32)
-        state = (nothing, nothing)
-        states = []
-        for block in range(levs):
-            states.append(state)
-            for entry in range(2):
-                state_send[block, entry] = state[entry]
-            if block < levs - 1:
-                slot = slot_of(block)
-                state = plus(apply(matrix(slot, 0), state), vector(slot, 0))
+        states = [(nothing, nothing)]
+        for block in range(levs - 1):
+            slot = slot_of(block)
+            states.append(plus(apply(matrix(slot, 0), states[-1]), vector(slot, 0)))
         state = (nothing, nothing)
         for block in range(levs - 1, -1, -1):
-            for entry in range(2):
-                state_send[block, 2 + entry] = state[entry]
+            for entry, value in enumerate(states[block] + state):
+                target[block, entry] = value
             if block:
                 slot = slot_of(block)
                 state = plus(
                     apply(matrix(slot, 1), state),
                     plus(apply(matrix(slot, 2), states[block]), vector(slot, 1)),
                 )
+
+    def send_back(source, target, sems):
         for offset in range(1, levs):
-            level_copy(state_send, state_recv, state_sems, offset, peer(offset)).start()
-        state_recv[0] = state_send[lev]
+            level_copy(source, target, sems, offset, peer(offset)).start()
+        target[0] = source[lev]
+
+    @pl.when(solver)
+    def _():
+        at_solver(block_send, block_recv, block_sems)
+        at_solver(carry_send, carry_recv, carry_sems)
+        solve(block_recv, carry_recv, state_send)
+        send_back(state_send, state_recv, state_sems)
+
+    @pl.when(opener)
+    def _():
+        pl.semaphore_wait(open_sem, 1)
+        to_side(edge_send, edge_recv, edge_sems, 0).start()
+        to_side(side_send, side_recv, side_sems, 0).start()
+        mend()
+
+    @pl.when(lev == chief)
+    def _():
+        at_chief(edge_block_send, edge_block_recv, edge_block_sems)
+        at_chief(extra_send, extra_recv, extra_sems)
+        solve(edge_block_recv, extra_recv, tail_send)
+        send_back(tail_send, tail_recv, tail_sems)
 
     for copy in side_copies:
         copy.wait_recv()
@@ -404,9 +523,10 @@
         def _():
             level_copy(state_send, state_recv, state_sems, offset, 0).wait_recv()
 
+
     def settle(index, carry):
         lane_part = part(index)
-        for band in range(rows // TILE_ROWS):
+        for band in range(bands):
             row_part = pl.ds(band * TILE_ROWS, TILE_ROWS)
 
             def gain(ref, level):
@@ -427,15 +547,48 @@
         return carry
 
     lax.fori_loop(0, halves, settle, 0)
+    for offset in range(1, levs):
+
+        @pl.when(lax.rem(lev + levs - offset, levs) == chief)
+        def _():
+            level_copy(tail_send, tail_recv, tail_sems, offset, 0).wait_recv()
+
+    entering = [tail_recv[slot_of(chief), place] for place in range(4)]
+    state = tuple(entering[:2])
+    falling = []
+    for level in range(levels):
+        fresh = tuple(narrow_forcing[place, level] for place in range(2))
+        state = plus(apply(narrow_matrix(1, level), state), fresh)
+        falling.append(state)
+    state = tuple(entering[2:])
+    for level in range(levels - 1, -1, -1):
+        state = plus(apply(narrow_matrix(2, level), state), falling[level])
+        for place, field in ((0, 2), (1, 4)):
+            for index in range(parts):
+                band, half = divmod(index, halves)
+                edge = band * (rows - 2)
+                stepped[
+                    field,
+                    level,
+                    edge : edge + 2,
+                    half * TILE_LANES : (half + 1) * TILE_LANES,
+                ] = state[place][2 * index : 2 * index + 2]
     for copy in edge_copies + side_copies:
         copy.wait_send()
     to_solvers(block_send, block_recv, block_sems, False)
     to_solvers(carry_send, carry_recv, carry_sems, False)
+    to_chief(edge_block_send, edge_block_recv, edge_block_sems, False)
+    to_chief(extra_send, extra_recv, extra_sems, False)
 
     @pl.when(solver)
     def _():
         for offset in range(1, levs):
             level_copy(state_send, state_recv, state_sems, offset, 0).wait_send()
+
+    @pl.when(lev == chief)
+    def _():
+        for offset in range(1, levs):
+            level_copy(tail_send, tail_recv, tail_sems, offset, 0).wait_send()
 
 
 def local(levs, tiles, adjoint, courant, metric, pivot_inverse, lower_gain, upper_gain):
@@ -455,13 +608,21 @@
         scratch_shapes=[vmem(*array.shape) for array in arrays]
         + [
             vmem(2, levels, rows, lanes),
-            vmem(2, 2, levels, 2, lanes),
-            vmem(2, 2, levels, 2, lanes),
+            vmem(3, 4, levels, *small),
+            vmem(2, levels, *small),
+            vmem(2, 2, levels, parts, TILE_LANES),
+            vmem(2, 2, levels, parts, TILE_LANES),
             vmem(2, 3, levels, 2, lanes),
             vmem(2, 3, levels, 2, lanes),
             vmem(parts, 12, *small),
             vmem(levs, 12, *small),
             vmem(parts, 4, *small),
+            vmem(levs, 4, *small),
+            vmem(levs, 4, *small),
+            vmem(levs, 4, *small),
+            vmem(12, *small),
+            vmem(levs, 12, *small),
+            vmem(4, *small),
             vmem(levs, 4, *small),
             vmem(levs, 4, *small),
             vmem(levs, 4, *small),
@@ -471,6 +632,10 @@
             pltpu.SemaphoreType.DMA((2, levs)),
             pltpu.SemaphoreType.DMA((2, levs)),
             pltpu.SemaphoreType.DMA((2, levs)),
+            pltpu.SemaphoreType.DMA((2, levs)),
+            pltpu.SemaphoreType.DMA((2, levs)),
+            pltpu.SemaphoreType.DMA((2, levs)),
+            pltpu.SemaphoreType.REGULAR,
         ],
         compiler_params=pltpu.CompilerParams(collective_id=0, has_side_effects=True),
     )(*arrays)

time: 29.6 us -> 28.3 us (0.956)
  Pallas kernels: 28.6 us -> 27.3 us
    pallas_call x1, Pallas kernels: 28.6 us -> 27.3 us  [local(): pl.pallas_call(functools.partial(kernel, levs, tiles), out_shape=pltpu.VM...]
where the time goes in v3:
time: 28.3 us; the launch traced here: 28.2 us
  Pallas kernels  27.3 us (96%)
  local copies, waits for them, and re-layouts  0.84 us (3%)
    pallas_call x1, Pallas kernels, local(): pl.pallas_call(functools.partial(kernel, levs, tiles), out_shape=pltpu.VM...  27.3 us
    unnamed x1, local copies, waits for them, and re-layouts  0.84 us

profile of v3, /device:TPU:1, one launch (start us, length us, event | category | flops | bytes accessed | tf_op | source)
XLA Modules:
  0.0 28.2 jit_solution(13780746019904298991)
XLA Ops:
  0.0 27.3 %shard_map.64 = f32[5,8,16,256]{3,2,1,0:T(8,128)S(1)} custom-call(f32[5,8,16,256]{3,2,1,0:T(8,128)} %adjoint_hbm.1, f32[2,8,16,256]{3,2,1,0:T(8,128)} %courant_hbm.1, f32[2,8,16,256]{3,2,1,0:T(8,128)} %metric_hbm.1, f32[4,8,16,256]{3,2,1,0:T(8,128)} %pivot_hbm.1, f32[4,8,16,256]{3,2,1,0:T(8,128)} %lower_hbm.1, f32[4,8,16,256]{3,2,1,0:T(8,128)} %upper_hbm.1), custom_call_target="tpu_custom_call" | custom-call | tf_op jit(solution)/shard_map/pallas_call | solution.py:603
  27.3 0.8 %copy.8 = f32[5,8,16,256]{3,2,1,0:T(8,128)} copy(f32[5,8,16,256]{3,2,1,0:T(8,128)S(1)} %shard_map.64) | data formatting | bytes 1310720

commit v4 on v3

--- a/solution.py
+++ b/solution.py
@@ -488,6 +488,37 @@
         to_side(side_send, side_recv, side_sems, 0).start()
         mend()
 
+    for offset in range(1, levs):
+
+        @pl.when(solves(lax.rem(lev + levs - offset, levs)))
+        def _():
+            level_copy(state_send, state_recv, state_sems, offset, 0).wait_recv()
+
+
+    def settle(index, carry):
+        lane_part = part(index)
+        for band in range(bands):
+            row_part = pl.ds(band * TILE_ROWS, TILE_ROWS)
+
+            def gain(ref, level):
+                return tuple(ref[entry, level, row_part, lane_part] for entry in range(4))
+
+            slot = slot_of(first + band * halves + index)
+            state = (state_recv[slot, 0], state_recv[slot, 1])
+            falling = []
+            for level in range(levels):
+                fresh = tuple(forcing[place, level, row_part, lane_part] for place in range(2))
+                state = plus(apply(gain(lower, level), state), fresh)
+                falling.append(state)
+            state = (state_recv[slot, 2], state_recv[slot, 3])
+            for level in range(levels - 1, -1, -1):
+                state = plus(apply(gain(upper, level), state), falling[level])
+                stepped[2, level, row_part, lane_part] = state[0]
+                stepped[4, level, row_part, lane_part] = state[1]
+        return carry
+
+    lax.fori_loop(0, halves, settle, 0)
+
     @pl.when(lev == chief)
     def _():
         at_chief(edge_block_send, edge_block_recv, edge_block_sems)
@@ -517,36 +548,6 @@
 
     lax.fori_loop(0, levels, finish, 0)
 
-    for offset in range(1, levs):
-
-        @pl.when(solves(lax.rem(lev + levs - offset, levs)))
-        def _():
-            level_copy(state_send, state_recv, state_sems, offset, 0).wait_recv()
-
-
-    def settle(index, carry):
-        lane_part = part(index)
-        for band in range(bands):
-            row_part = pl.ds(band * TILE_ROWS, TILE_ROWS)
-
-            def gain(ref, level):
-                return tuple(ref[entry, level, row_part, lane_part] for entry in range(4))
-
-            slot = slot_of(first + band * halves + index)
-            state = (state_recv[slot, 0], state_recv[slot, 1])
-            falling = []
-            for level in range(levels):
-                fresh = tuple(forcing[place, level, row_part, lane_part] for place in range(2))
-                state = plus(apply(gain(lower, level), state), fresh)
-                falling.append(state)
-            state = (state_recv[slot, 2], state_recv[slot, 3])
-            for level in range(levels - 1, -1, -1):
-                state = plus(apply(gain(upper, level), state), falling[level])
-                stepped[2, level, row_part, lane_part] = state[0]
-                stepped[4, level, row_part, lane_part] = state[1]
-        return carry
-
-    lax.fori_loop(0, halves, settle, 0)
     for offset in range(1, levs):
 
         @pl.when(lax.rem(lev + levs - offset, levs) == chief)

time: 28.3 us -> 28.3 us (level)
  no operation moved by 1% of the time
where the time goes in v4:
time: 28.3 us; the launch traced here: 28.2 us
  Pallas kernels  27.3 us (96%)
  local copies, waits for them, and re-layouts  0.84 us (3%)
    pallas_call x1, Pallas kernels, local(): pl.pallas_call(functools.partial(kernel, levs, tiles), out_shape=pltpu.VM...  27.3 us
    unnamed x1, local copies, waits for them, and re-layouts  0.84 us

profile of v4, /device:TPU:1, one launch (start us, length us, event | category | flops | bytes accessed | tf_op | source)
XLA Modules:
  0.0 28.2 jit_solution(11217213428646224990)
XLA Ops:
  0.0 27.3 %shard_map.64 = f32[5,8,16,256]{3,2,1,0:T(8,128)S(1)} custom-call(f32[5,8,16,256]{3,2,1,0:T(8,128)} %adjoint_hbm.1, f32[2,8,16,256]{3,2,1,0:T(8,128)} %courant_hbm.1, f32[2,8,16,256]{3,2,1,0:T(8,128)} %metric_hbm.1, f32[4,8,16,256]{3,2,1,0:T(8,128)} %pivot_hbm.1, f32[4,8,16,256]{3,2,1,0:T(8,128)} %lower_hbm.1, f32[4,8,16,256]{3,2,1,0:T(8,128)} %upper_hbm.1), custom_call_target="tpu_custom_call" | custom-call | tf_op jit(solution)/shard_map/pallas_call | solution.py:604
  27.3 0.8 %copy.8 = f32[5,8,16,256]{3,2,1,0:T(8,128)} copy(f32[5,8,16,256]{3,2,1,0:T(8,128)S(1)} %shard_map.64) | data formatting | bytes 1310720
